TPU v7x, 32 devices: a whole 2x2x4 slice. The times are simulated.
32 devices in a mesh: dp: 4 (over z), adapter: 8 (over y, x, core).
Axes of the slice: x: 2, y: 2, z: 4, core: 2. Of those that a mesh axis runs over, the one named last changes fastest.
Arguments:
- states: bfloat16 [2, 1024, 8192], P(None, ('dp', 'adapter')), may hold values from -6 to 6
- request_slot_index: int32 [2, 1024, 1], P(None, ('dp', 'adapter')), may hold values from 0 to 7; in each aligned block of 32 rows (0 to 31, 32 to 63, ..., all dimensions but the last counted through in order) at most 8 rows name the same one
- down_weights: bfloat16 [32, 64, 8192], P(('dp', 'adapter')), may hold values from -0.0625 to 0.0625
- up_weights: bfloat16 [32, 64, 8192], P(('dp', 'adapter')), may hold values from -0.75 to 0.75
- active_adapter_owner: int32 [2, 8], replicated, may hold values from 0 to 3
Outputs:
- delta: bfloat16 [2, 1024, 8192], P(None, ('dp', 'adapter'))
Inputs may be any that keep to these rules, and one draw needn't show every extreme that they name: `request_slot_index`: within the rows of one device at one step (aligned blocks of 32 rows), no column is named by more than 8 rows, a bound that some block reaches.
All inputs are finite; a program needn't handle non-finite values.
Results may differ from a plain program's by a relative error of at most 0.0049.
Values may be sent and summed in bfloat16 or wider, within the bound.
A program may use at most 64 MiB of HBM per device.

v0:
```python
import jax
import jax.numpy as jnp
from jax import lax
from jax.sharding import PartitionSpec as P


def from_root(array, axis, root):
    mine = lax.axis_index(axis) == root
    return lax.psum(jnp.where(mine, array, jnp.zeros_like(array)), axis)


def slot_matrix(column_ids, columns, capacity):
    hits = (column_ids[:, None] == jnp.arange(columns, dtype=jnp.int32)[None, :]).astype(jnp.int32)
    slot_rank = jnp.sum(jnp.cumsum(hits, axis=0) * hits, axis=1) - 1
    target = column_ids * capacity + slot_rank
    return (target[:, None] == jnp.arange(columns * capacity, dtype=jnp.int32)[None, :]).astype(
        jnp.bfloat16
    )


def project(arrived, stack_down, stack_up):
    low_rank = jnp.einsum(
        "scnd,srd->scnr", arrived, stack_down, preferred_element_type=jnp.float32
    ).astype(jnp.bfloat16)
    return jnp.einsum(
        "scnr,srd->scnd", low_rank, stack_up, preferred_element_type=jnp.float32
    ).astype(jnp.bfloat16)


def serve_one(arrived, stack_down, stack_up):
    result = project(arrived, stack_down, stack_up)
    return lax.all_to_all(result, "adapter", split_axis=1, concat_axis=1, tiled=True)


def body(states, request_slot_index, down_weights, up_weights, active_adapter_owner):
    step_count = states.shape[0]
    rows_dev = states.shape[1]
    model_width = states.shape[2]
    columns = lax.axis_size("adapter")
    column_index = lax.axis_index("adapter")
    capacity = max(2, 2 * rows_dev // columns)
    slot_count = columns * capacity
    downs = []
    uppers = []
    for step_index in range(step_count):
        owner_leader = active_adapter_owner[step_index, column_index]
        got_down, got_up = (
            from_root(down_weights[0], "dp", owner_leader),
            from_root(up_weights[0], "dp", owner_leader),
        )
        downs.append(got_down)
        uppers.append(got_up)
    stack_down = jnp.stack(downs)
    stack_up = jnp.stack(uppers)
    placements = []
    outgoing_list = []
    for step_index in range(step_count):
        placement = slot_matrix(request_slot_index[step_index, :, 0], columns, capacity)
        placements.append(placement)
        packed = lax.dot_general(
            placement,
            states[step_index],
            (((0,), (0,)), ((), ())),
            preferred_element_type=jnp.float32,
        )
        outgoing_list.append(packed.astype(jnp.bfloat16).reshape(columns, capacity, model_width))
    outgoing = jnp.stack(outgoing_list)
    returned_list = []
    for step_index in range(step_count):
        returned_list.append(
            serve_one(
                lax.all_to_all(
                    outgoing[step_index : step_index + 1],
                    "adapter",
                    split_axis=1,
                    concat_axis=1,
                    tiled=True,
                ),
                stack_down=stack_down[step_index : step_index + 1],
                stack_up=stack_up[step_index : step_index + 1],
            )
        )
    returned_rows = jnp.concatenate(returned_list, axis=0)
    delta_list = []
    for step_index in range(step_count):
        flat_rows = returned_rows[step_index].reshape(slot_count, model_width)
        delta_list.append(
            jnp.dot(placements[step_index], flat_rows, preferred_element_type=jnp.float32).astype(
                jnp.bfloat16
            )
        )
    return jnp.stack(delta_list)


def solution(mesh):
    return jax.shard_map(
        body,
        mesh=mesh,
        in_specs=(
            P(None, ("dp", "adapter"), None),
            P(None, ("dp", "adapter"), None),
            P(("dp", "adapter"), None, None),
            P(("dp", "adapter"), None, None),
            P(),
        ),
        out_specs=P(None, ("dp", "adapter"), None),
        check_vma=False,
    )
```

profile of v0, /device:TPU:0, one launch (start us, length us, event | category | flops | bytes accessed | tf_op | source)
XLA Modules:
  0.0 222.1 jit_solution(10519682711103507936)
XLA Ops:
  6.5 0.0 all-reduce.3.cloned.1.call-start
  6.5 1.4 constant_dynamic-slice_fusion.1
  9.3 3.7 %select_bitcast_fusion.2 = (bf16[64,8192]{1,0:T(8,128)(2,1)}, bf16[64,8192]{1,0:T(8,128)(2,1)}, bf16[64,8192]{1,0:T(8,128)(2,1)}, bf16[64,8192]{1,0:T(8,128)(2,1)}) fusion(bf16[1,64,8192]{2,1,0:T(8,128)(2,1)} %param.8, pred[]{:T(512)S(6)} %eq.66, pred[]{:T(512)S(6)} %eq.73, bf16[1,64,8192]{2,1,0:T(8,128)(2,1)} %param.7), kind=kLoop, calls=%fused_computation.25 | loop fusion | flops 2097152 | bytes 6291458 | tf_op jit(solution)/shard_map/jit(_where)/select_n | solution.py:9
  13.0 0.0 copy-start.2
  13.0 0.0 copy-start
  13.0 0.0 all-reduce.3.cloned.1.call-update
  13.0 0.7 copy-done.2
  13.6 0.1 fusion.23
  13.7 0.1 reduce_window_sum.17
  13.8 0.1 fusion.22
  13.8 0.1 reduce_window_sum.18
  13.9 0.2 select_reduce_fusion
  14.1 0.1 copy-done
  14.2 1.6 fusion
  15.8 5.2 %all-to-all-start = ((bf16[1,8,8,8192]{3,2,0,1:T(8,128)(2,1)}), bf16[1,8,8,8192]{3,2,0,1:T(8,128)(2,1)S(1)}, u32[]{:S(2)}, u32[]{:S(2)}) async-start(bf16[1,8,8,8192]{3,2,0,1:T(8,128)(2,1)} %fusion), calls=%async_computation | async-start | bytes 2097152 | tf_op jit(solution)/shard_map/all_to_all | solution.py:72
  21.0 1.6 fusion.2
  22.5 13.8 %all-to-all-done = bf16[1,8,8,8192]{3,2,0,1:T(8,128)(2,1)S(1)} async-done(((bf16[1,8,8,8192]{3,2,0,1:T(8,128)(2,1)}), bf16[1,8,8,8192]{3,2,0,1:T(8,128)(2,1)S(1)}, u32[]{:S(2)}, u32[]{:S(2)}) %all-to-all-start) | async-done | bytes 1048608 | tf_op jit(solution)/shard_map/all_to_all | solution.py:72
  36.4 3.6 %all-to-all-start.2 = ((bf16[1,8,8,8192]{3,2,0,1:T(8,128)(2,1)}), bf16[1,8,8,8192]{3,2,0,1:T(8,128)(2,1)S(1)}, u32[]{:S(2)}, u32[]{:S(2)}) async-start(bf16[1,8,8,8192]{3,2,0,1:T(8,128)(2,1)} %fusion.2), calls=%async_computation.2 | async-start | bytes 2097152 | tf_op jit(solution)/shard_map/all_to_all | solution.py:72
  39.9 131.9 %all-reduce.3.cloned.1.call-done = (bf16[64,8192]{1,0:T(8,128)(2,1)}, bf16[64,8192]{1,0:T(8,128)(2,1)}, bf16[64,8192]{1,0:T(8,128)(2,1)}, bf16[64,8192]{1,0:T(8,128)(2,1)}) async-done(((bf16[64,8192]{1,0:T(8,128)(2,1)}, bf16[64,8192]{1,0:T(8,128)(2,1)}, bf16[64,8192]{1,0:T(8,128)(2,1)}, bf16[64,8192]{1,0:T(8,128)(2,1)}), (bf16[64,8192]{1,0:T(8,128)(2,1)}, bf16[64,8192]{1,0:T(8,128)(2,1)}, ...) | async-done | bytes 4194320 | tf_op jit(solution)/shard_map/psum | solution.py:9
  171.9 3.8 %fusion.1 = bf16[1,8,8,8192]{3,2,0,1:T(8,128)(2,1)} fusion(bf16[64,8192]{1,0:T(8,128)(2,1)} %get-tuple-element.7, bf16[64,8192]{1,0:T(8,128)(2,1)} %get-tuple-element.8, bf16[1,8,8,8192]{3,2,0,1:T(8,128)(2,1)S(1)} %all-to-all-done), kind=kOutput, calls=%fused_computation.5 | convolution fusion | flops 134746112 | bytes 4194304 | tf_op jit(solution)/shard_map/scnr,srd->scnd/dot_general | solution.py:25
  175.7 0.0 copy-start.1
  175.7 0.0 all-to-all-done.2
  175.7 3.8 %all-to-all-start.1 = ((bf16[1,8,8,8192]{3,2,0,1:T(8,128)(2,1)}), bf16[1,8,8,8192]{3,2,0,1:T(8,128)(2,1)S(1)}, u32[]{:S(2)}, u32[]{:S(2)}) async-start(bf16[1,8,8,8192]{3,2,0,1:T(8,128)(2,1)} %fusion.1), calls=%async_computation.1 | async-start | bytes 2097152 | tf_op jit(solution)/shard_map/all_to_all | solution.py:32
  179.5 0.0 copy-done.1
  179.5 3.5 %fusion.3 = bf16[1,8,8,8192]{3,2,0,1:T(8,128)(2,1)} fusion(bf16[64,8192]{1,0:T(8,128)(2,1)S(1)} %copy-done.1, bf16[64,8192]{1,0:T(8,128)(2,1)} %get-tuple-element.6, bf16[1,8,8,8192]{3,2,0,1:T(8,128)(2,1)S(1)} %all-to-all-done.2), kind=kOutput, calls=%fused_computation.7 | convolution fusion | flops 134746112 | bytes 4194304 | tf_op jit(solution)/shard_map/scnr,srd->scnd/dot_general | solution.py:25
  183.0 11.9 %all-to-all-done.1 = bf16[1,8,8,8192]{3,2,0,1:T(8,128)(2,1)S(1)} async-done(((bf16[1,8,8,8192]{3,2,0,1:T(8,128)(2,1)}), bf16[1,8,8,8192]{3,2,0,1:T(8,128)(2,1)S(1)}, u32[]{:S(2)}, u32[]{:S(2)}) %all-to-all-start.1) | async-done | bytes 1048608 | tf_op jit(solution)/shard_map/all_to_all | solution.py:32
  194.9 3.6 %all-to-all-start.3 = ((bf16[1,8,8,8192]{3,2,0,1:T(8,128)(2,1)}), bf16[1,8,8,8192]{3,2,0,1:T(8,128)(2,1)S(1)}, u32[]{:S(2)}, u32[]{:S(2)}) async-start(bf16[1,8,8,8192]{3,2,0,1:T(8,128)(2,1)} %fusion.3), calls=%async_computation.3 | async-start | bytes 2097152 | tf_op jit(solution)/shard_map/all_to_all | solution.py:32
  198.5 0.4 fusion.4
  198.9 15.0 %all-to-all-done.3 = bf16[1,8,8,8192]{3,2,0,1:T(8,128)(2,1)S(1)} async-done(((bf16[1,8,8,8192]{3,2,0,1:T(8,128)(2,1)}), bf16[1,8,8,8192]{3,2,0,1:T(8,128)(2,1)S(1)}, u32[]{:S(2)}, u32[]{:S(2)}) %all-to-all-start.3) | async-done | bytes 1048608 | tf_op jit(solution)/shard_map/all_to_all | solution.py:32
  213.8 0.3 fusion.5
  214.2 1.1 pad_maximum_fusion
  (2 shorter events, 0.0 us)
Async XLA Ops:
  6.5 165.3 %all-reduce.3.cloned.1.call-start = ((), (), s32[]{:S(2)}) async-start(), calls=%async_computation.4 | async-start | bytes 8388608 | tf_op jit(solution)/shard_map/psum | solution.py:9
  13.0 0.7 copy-start.2
  13.0 1.2 copy-start
  15.8 20.6 %all-to-all-start = ((bf16[1,8,8,8192]{3,2,0,1:T(8,128)(2,1)}), bf16[1,8,8,8192]{3,2,0,1:T(8,128)(2,1)S(1)}, u32[]{:S(2)}, u32[]{:S(2)}) async-start(bf16[1,8,8,8192]{3,2,0,1:T(8,128)(2,1)} %fusion), calls=%async_computation | async-start | bytes 2097152 | tf_op jit(solution)/shard_map/all_to_all | solution.py:72
  36.4 139.3 %all-to-all-start.2 = ((bf16[1,8,8,8192]{3,2,0,1:T(8,128)(2,1)}), bf16[1,8,8,8192]{3,2,0,1:T(8,128)(2,1)S(1)}, u32[]{:S(2)}, u32[]{:S(2)}) async-start(bf16[1,8,8,8192]{3,2,0,1:T(8,128)(2,1)} %fusion.2), calls=%async_computation.2 | async-start | bytes 2097152 | tf_op jit(solution)/shard_map/all_to_all | solution.py:72
  175.7 3.8 %copy-start.1 = (bf16[64,8192]{1,0:T(8,128)(2,1)S(1)}, bf16[64,8192]{1,0:T(8,128)(2,1)}, u32[]{:S(2)}) copy-start(bf16[64,8192]{1,0:T(8,128)(2,1)} %get-tuple-element.5) | copy-start | bytes 3145732
  175.7 19.2 %all-to-all-start.1 = ((bf16[1,8,8,8192]{3,2,0,1:T(8,128)(2,1)}), bf16[1,8,8,8192]{3,2,0,1:T(8,128)(2,1)S(1)}, u32[]{:S(2)}, u32[]{:S(2)}) async-start(bf16[1,8,8,8192]{3,2,0,1:T(8,128)(2,1)} %fusion.1), calls=%async_computation.1 | async-start | bytes 2097152 | tf_op jit(solution)/shard_map/all_to_all | solution.py:32
  194.9 18.9 %all-to-all-start.3 = ((bf16[1,8,8,8192]{3,2,0,1:T(8,128)(2,1)}), bf16[1,8,8,8192]{3,2,0,1:T(8,128)(2,1)S(1)}, u32[]{:S(2)}, u32[]{:S(2)}) async-start(bf16[1,8,8,8192]{3,2,0,1:T(8,128)(2,1)} %fusion.3), calls=%async_computation.3 | async-start | bytes 2097152 | tf_op jit(solution)/shard_map/all_to_all | solution.py:32
Sparse Core Ops, SparseCore 0:
  13.1 158.7 all-reduce.2
where the time goes:
time: 223 us; the launch traced here: 222 us
  waiting for transfers between devices  173 us (78%)
  starting transfers between devices  16.1 us (7%)
  between operations  14.8 us (7%)
  matrix products  11.2 us (5%)
  other arithmetic  5.16 us (2%)
    psum x1, waiting for transfers between devices, from_root(): return lax.psum(jnp.where(mine, array, jnp.zeros_like(array)), axis)  132 us
    all_to_all x2, waiting for transfers between devices, serve_one(): lax.all_to_all(result, 'adapter', split_axis=1, concat_axis=1, tiled=True)  26.9 us
    all_to_all x2, waiting for transfers between devices, body(): lax.all_to_all(outgoing[step_index:step_index + 1], 'adapter', split_axis...  13.9 us
    all_to_all x2, starting transfers between devices, body(): lax.all_to_all(outgoing[step_index:step_index + 1], 'adapter', split_axis...  8.73 us
    all_to_all x2, starting transfers between devices, serve_one(): lax.all_to_all(result, 'adapter', split_axis=1, concat_axis=1, tiled=True)  7.39 us
    dot_general x2, matrix products, project(): jnp.einsum('scnr,srd->scnd', low_rank, stack_up, preferred_element_type=j...  7.33 us
  transfers between devices with their start and end apart: 5, of which 4 were waited for; matrix products, arithmetic and copies ran while one was open for 5% of the time, Pallas kernels for 0%

commit v1 on v0

--- a/solution.py
+++ b/solution.py
@@ -2,6 +2,29 @@
 import jax.numpy as jnp
 from jax import lax
 from jax.sharding import PartitionSpec as P
+
+
+def cut_along(x, dim, size):
+    shape = x.shape
+    pieces = x.reshape(*shape[:dim], size, shape[dim] // size, *shape[dim + 1 :])
+    return jnp.moveaxis(pieces, dim, 0)
+
+
+def joined_along(blocks, dim):
+    lengths = list(blocks.shape[1:])
+    lengths[dim] *= blocks.shape[0]
+    return jnp.moveaxis(blocks, 0, dim).reshape(lengths)
+
+
+def exchange_directly(value, axis, split_dim, concat_dim):
+    devices, position = (lax.axis_size(axis), lax.axis_index(axis))
+    pieces = cut_along(value, split_dim, devices)
+    outs = [pieces[position]]
+    for step in range(1, devices):
+        sent = pieces[(position + step) % devices]
+        outs.append(lax.ppermute(sent, axis, [(i, (i + step) % devices) for i in range(devices)]))
+    pieces = jnp.stack(outs)[(position - jnp.arange(devices)) % devices]
+    return joined_along(pieces, concat_dim)
 
 
 def from_root(array, axis, root):
@@ -69,13 +92,7 @@
     for step_index in range(step_count):
         returned_list.append(
             serve_one(
-                lax.all_to_all(
-                    outgoing[step_index : step_index + 1],
-                    "adapter",
-                    split_axis=1,
-                    concat_axis=1,
-                    tiled=True,
-                ),
+                exchange_directly(outgoing[step_index : step_index + 1], "adapter", 1, 1),
                 stack_down=stack_down[step_index : step_index + 1],
                 stack_up=stack_up[step_index : step_index + 1],
             )

time: 223 us -> 230 us (1.031)
  starting transfers between devices: 16.1 us -> 22.6 us
  local copies, waits for them, and re-layouts: 2.18 us -> 7.4 us
  waiting for transfers between devices: 173 us -> 169 us
    ppermute x0 -> x14, starting transfers between devices: none -> 15.4 us  [exchange_directly(): lax.ppermute(sent, axis, [(i, (i + step) % devices) for i in range(device...]
    all_to_all x2 -> x0, waiting for transfers between devices: 13.9 us -> none  [body(): lax.all_to_all(outgoing[step_index:step_index + 1], 'adapter', split_axis...]
    all_to_all x2 -> x0, starting transfers between devices: 8.73 us -> none  [body(): lax.all_to_all(outgoing[step_index:step_index + 1], 'adapter', split_axis...]
    ppermute x0 -> x14, waiting for transfers between devices: none -> 7.3 us  [exchange_directly(): lax.ppermute(sent, axis, [(i, (i + step) % devices) for i in range(device...]
    psum x1, waiting for transfers between devices: 132 us -> 136 us  [from_root(): return lax.psum(jnp.where(mine, array, jnp.zeros_like(array)), axis)]
    unnamed x6 -> x18, local copies, waits for them, and re-layouts: 0.76 us -> 3.18 us
  transfers between devices with their start and end apart: 5 -> 17, of which waited for: 4 -> 8; matrix products, arithmetic and copies ran while one was open for 5% -> 7% of each run, Pallas kernels for 0% -> 0%
where the time goes in v1:
time: 230 us
  waiting for transfers between devices  169 us (73%)
  starting transfers between devices  22.6 us (10%)
  between operations  15 us (7%)
  matrix products  10.5 us (5%)
  local copies, waits for them, and re-layouts  7.4 us (3%)
  other arithmetic  5.52 us (2%)
    psum x1, waiting for transfers between devices, from_root(): return lax.psum(jnp.where(mine, array, jnp.zeros_like(array)), axis)  136 us
    all_to_all x2, waiting for transfers between devices, serve_one(): lax.all_to_all(result, 'adapter', split_axis=1, concat_axis=1, tiled=True)  25.9 us
    ppermute x14, starting transfers between devices, exchange_directly(): lax.ppermute(sent, axis, [(i, (i + step) % devices) for i in range(device...  15.4 us
    dot_general x2, matrix products, project(): jnp.einsum('scnr,srd->scnd', low_rank, stack_up, preferred_element_type=j...  7.64 us
    ppermute x14, waiting for transfers between devices, exchange_directly(): lax.ppermute(sent, axis, [(i, (i + step) % devices) for i in range(device...  7.3 us
    all_to_all x2, starting transfers between devices, serve_one(): lax.all_to_all(result, 'adapter', split_axis=1, concat_axis=1, tiled=True)  7.25 us
  transfers between devices with their start and end apart: 17, of which 8 were waited for; matrix products, arithmetic and copies ran while one was open for 7% of the time, Pallas kernels for 0%

profile of v1, /device:TPU:0, one launch (start us, length us, event | category | flops | bytes accessed | tf_op | source)
XLA Modules:
  0.0 229.9 jit_solution(15577797425762858136)
XLA Ops:
  6.5 0.7 slice_bitcast_fusion.1
  7.2 0.1 fusion.18
  7.3 0.1 reduce_window_sum.18
  7.3 0.1 fusion.19
  7.4 0.1 reduce_window_sum.17
  7.5 0.2 select_reduce_fusion
  7.7 0.7 add_add_fusion.1
  8.3 1.6 fusion.2
  10.0 0.9 dynamic-slice_bitcast_fusion
  10.9 0.5 collective-permute-start.7
  11.3 2.5 %collective-permute-start.8 = (bf16[1,1,8,8192]{3,2,1,0:T(8,128)(2,1)}, bf16[1,1,8,8192]{3,2,1,0:T(8,128)(2,1)}, u32[]{:S(2)}, u32[]{:S(2)}) collective-permute-start(bf16[1,1,8,8192]{3,2,1,0:T(8,128)(2,1)} %get-tuple-element.22), channel_id=1, source_target_pairs={{0,2},{1,3},{2,4},{3,5},{4,6},{5,7},{6,0},{7,1},{8,10},{9,11},{10,... | collective-permute-start | bytes 393224 | tf_op jit(solution)/shard_map/ppermute | solution.py:25
  13.9 2.4 %collective-permute-start.9 = (bf16[1,1,8,8192]{3,2,1,0:T(8,128)(2,1)}, bf16[1,1,8,8192]{3,2,1,0:T(8,128)(2,1)S(1)}, u32[]{:S(2)}, u32[]{:S(2)}) collective-permute-start(bf16[1,1,8,8192]{3,2,1,0:T(8,128)(2,1)} %get-tuple-element.21), channel_id=1, source_target_pairs={{0,3},{1,4},{2,5},{3,6},{4,7},{5,0},{6,1},{7,2},{8,11},{9,12},{10,... | collective-permute-start | bytes 393224 | tf_op jit(solution)/shard_map/ppermute | solution.py:25
  16.2 0.5 collective-permute-start.10
  16.7 0.1 collective-permute-start.11
  16.8 0.7 constant_dynamic-slice_fusion
  18.9 3.3 %select_bitcast_fusion.2 = (bf16[64,8192]{1,0:T(8,128)(2,1)}, bf16[64,8192]{1,0:T(8,128)(2,1)}, bf16[64,8192]{1,0:T(8,128)(2,1)}, bf16[64,8192]{1,0:T(8,128)(2,1)}) fusion(bf16[1,64,8192]{2,1,0:T(8,128)(2,1)S(1)} %copy-done.1, pred[]{:T(512)S(6)} %eq.84, pred[]{:T(512)S(6)} %eq.91, bf16[1,64,8192]{2,1,0:T(8,128)(2,1)} %param.7), kind=kLoop, calls=%fused_computation.25 | loop fusion | flops 2097152 | bytes 6291458 | tf_op jit(solution)/shard_map/jit(_where)/select_n | solution.py:32
  22.2 0.0 all-reduce.3.cloned.1.call-update
  22.2 1.2 copy-done
  23.4 0.5 fusion
  23.9 0.8 dynamic-slice_bitcast_fusion.7
  24.7 1.5 collective-permute-start.12
  26.2 0.9 bitcast_dynamic-update-slice_fusion.6
  27.1 2.4 %collective-permute-start.13 = (bf16[1,1,8,8192]{3,2,1,0:T(8,128)(2,1)S(1)}, bf16[1,1,8,8192]{3,2,1,0:T(8,128)(2,1)S(1)}, u32[]{:S(2)}, u32[]{:S(2)}) collective-permute-start(bf16[1,1,8,8192]{3,2,1,0:T(8,128)(2,1)S(1)} %get-tuple-element.17), channel_id=1, source_target_pairs={{0,7},{1,0},{2,1},{3,2},{4,3},{5,4},{6,5},{7,6},{8,15},{9,8},{10,9... | collective-permute-start | bytes 393224 | tf_op jit(solution)/shard_map/ppermute | solution.py:25
  29.5 1.0 bitcast_dynamic-update-slice_fusion.5
  30.5 0.1 collective-permute-start
  30.6 0.6 collective-permute-start.1
  31.2 1.4 collective-permute-start.2
  32.7 1.6 collective-permute-start.3
  34.3 0.1 collective-permute-start.4
  34.4 2.3 %collective-permute-done = bf16[1,1,8,8192]{3,2,1,0:T(8,128)(2,1)S(1)} collective-permute-done((bf16[1,1,8,8192]{3,2,1,0:T(8,128)(2,1)S(1)}, bf16[1,1,8,8192]{3,2,1,0:T(8,128)(2,1)S(1)}, u32[]{:S(2)}, u32[]{:S(2)}) %collective-permute-start) | collective-permute-done | bytes 131104 | tf_op jit(solution)/shard_map/ppermute | solution.py:25
  36.7 0.2 collective-permute-start.5
  36.9 1.0 collective-permute-done.1
  38.0 1.6 collective-permute-start.6
  39.6 3.2 %collective-permute-done.2 = bf16[1,1,8,8192]{3,2,1,0:T(8,128)(2,1)S(1)} collective-permute-done((bf16[1,1,8,8192]{3,2,1,0:T(8,128)(2,1)S(1)}, bf16[1,1,8,8192]{3,2,1,0:T(8,128)(2,1)S(1)}, u32[]{:S(2)}, u32[]{:S(2)}) %collective-permute-start.2) | collective-permute-done | bytes 131104 | tf_op jit(solution)/shard_map/ppermute | solution.py:25
  42.8 0.2 collective-permute-done.3
  43.0 0.5 collective-permute-done.4
  43.5 0.6 gather_fusion.1
  44.2 135.7 %all-reduce.3.cloned.1.call-done = (bf16[64,8192]{1,0:T(8,128)(2,1)}, bf16[64,8192]{1,0:T(8,128)(2,1)}, bf16[64,8192]{1,0:T(8,128)(2,1)}, bf16[64,8192]{1,0:T(8,128)(2,1)}) async-done(((bf16[64,8192]{1,0:T(8,128)(2,1)}, bf16[64,8192]{1,0:T(8,128)(2,1)}, bf16[64,8192]{1,0:T(8,128)(2,1)}, bf16[64,8192]{1,0:T(8,128)(2,1)}), (bf16[64,8192]{1,0:T(8,128)(2,1)}, bf16[64,8192]{1,0:T(8,128)(2,1)}, ...) | async-done | bytes 4194320 | tf_op jit(solution)/shard_map/psum | solution.py:32
  179.8 3.8 %fusion.3 = bf16[1,8,8,8192]{3,2,0,1:T(8,128)(2,1)} fusion(bf16[64,8192]{1,0:T(8,128)(2,1)} %get-tuple-element.5, bf16[8,8,8192]{2,1,0:T(8,128)(2,1)S(1)} %gather_fusion.1, bf16[64,8192]{1,0:T(8,128)(2,1)} %get-tuple-element.6), kind=kOutput, calls=%fused_computation.9 | convolution fusion | flops 134746112 | bytes 4194304 | tf_op jit(solution)/shard_map/scnr,srd->scnd/dot_general | solution.py:48
  183.6 3.7 %all-to-all-start.1 = ((bf16[1,8,8,8192]{3,2,0,1:T(8,128)(2,1)}), bf16[1,8,8,8192]{3,2,0,1:T(8,128)(2,1)S(1)}, u32[]{:S(2)}, u32[]{:S(2)}) async-start(bf16[1,8,8,8192]{3,2,0,1:T(8,128)(2,1)} %fusion.3), calls=%async_computation.1 | async-start | bytes 2097152 | tf_op jit(solution)/shard_map/all_to_all | solution.py:55
  187.4 0.6 gather_fusion
  188.0 3.8 %fusion.1 = bf16[1,8,8,8192]{3,2,0,1:T(8,128)(2,1)} fusion(bf16[64,8192]{1,0:T(8,128)(2,1)} %get-tuple-element.7, bf16[8,8,8192]{2,1,0:T(8,128)(2,1)S(1)} %gather_fusion, bf16[64,8192]{1,0:T(8,128)(2,1)} %get-tuple-element.8), kind=kOutput, calls=%fused_computation.7 | convolution fusion | flops 134746112 | bytes 4194304 | tf_op jit(solution)/shard_map/scnr,srd->scnd/dot_general | solution.py:48
  191.8 10.9 %all-to-all-done.1 = bf16[1,8,8,8192]{3,2,0,1:T(8,128)(2,1)S(1)} async-done(((bf16[1,8,8,8192]{3,2,0,1:T(8,128)(2,1)}), bf16[1,8,8,8192]{3,2,0,1:T(8,128)(2,1)S(1)}, u32[]{:S(2)}, u32[]{:S(2)}) %all-to-all-start.1) | async-done | bytes 1048608 | tf_op jit(solution)/shard_map/all_to_all | solution.py:55
  202.7 3.6 %all-to-all-start = ((bf16[1,8,8,8192]{3,2,0,1:T(8,128)(2,1)}), bf16[1,8,8,8192]{3,2,0,1:T(8,128)(2,1)S(1)}, u32[]{:S(2)}, u32[]{:S(2)}) async-start(bf16[1,8,8,8192]{3,2,0,1:T(8,128)(2,1)} %fusion.1), calls=%async_computation | async-start | bytes 2097152 | tf_op jit(solution)/shard_map/all_to_all | solution.py:55
  206.3 0.4 fusion.5
  206.7 15.0 %all-to-all-done = bf16[1,8,8,8192]{3,2,0,1:T(8,128)(2,1)S(1)} async-done(((bf16[1,8,8,8192]{3,2,0,1:T(8,128)(2,1)}), bf16[1,8,8,8192]{3,2,0,1:T(8,128)(2,1)S(1)}, u32[]{:S(2)}, u32[]{:S(2)}) %all-to-all-start) | async-done | bytes 1048608 | tf_op jit(solution)/shard_map/all_to_all | solution.py:55
  221.7 0.3 fusion.4
  222.0 1.1 pad_maximum_fusion
  (29 shorter events, 0.2 us)
Async XLA Ops:
  6.5 173.3 %all-reduce.3.cloned.1.call-start = ((), (), s32[]{:S(2)}) async-start(), calls=%async_computation.2 | async-start | bytes 8388608 | tf_op jit(solution)/shard_map/psum | solution.py:32
  10.0 6.9 %copy-start.2 = (s32[2,8]{1,0:T(2,128)S(1)}, s32[2,8]{1,0:T(2,128)}, u32[]{:S(2)}) copy-start(s32[2,8]{1,0:T(2,128)} %param.9) | copy-start | bytes 196
  10.0 8.9 %copy-start.1 = (bf16[1,64,8192]{2,1,0:T(8,128)(2,1)S(1)}, bf16[1,64,8192]{2,1,0:T(8,128)(2,1)}, u32[]{:S(2)}) copy-start(bf16[1,64,8192]{2,1,0:T(8,128)(2,1)} %param.8) | copy-start | bytes 3145732
  10.9 13.8 %collective-permute-start.7 = (bf16[1,1,8,8192]{3,2,1,0:T(8,128)(2,1)}, bf16[1,1,8,8192]{3,2,1,0:T(8,128)(2,1)}, u32[]{:S(2)}, u32[]{:S(2)}) collective-permute-start(bf16[1,1,8,8192]{3,2,1,0:T(8,128)(2,1)} %get-tuple-element.23), channel_id=1, source_target_pairs={{0,1},{1,2},{2,3},{3,4},{4,5},{5,6},{6,7},{7,0},{8,9},{9,10},{10,1... | collective-permute-start | bytes 393224 | tf_op jit(solution)/shard_map/ppermute | solution.py:25
  11.3 15.8 %collective-permute-start.8 = (bf16[1,1,8,8192]{3,2,1,0:T(8,128)(2,1)}, bf16[1,1,8,8192]{3,2,1,0:T(8,128)(2,1)}, u32[]{:S(2)}, u32[]{:S(2)}) collective-permute-start(bf16[1,1,8,8192]{3,2,1,0:T(8,128)(2,1)} %get-tuple-element.22), channel_id=1, source_target_pairs={{0,2},{1,3},{2,4},{3,5},{4,6},{5,7},{6,0},{7,1},{8,10},{9,11},{10,... | collective-permute-start | bytes 393224 | tf_op jit(solution)/shard_map/ppermute | solution.py:25
  13.9 16.6 %collective-permute-start.9 = (bf16[1,1,8,8192]{3,2,1,0:T(8,128)(2,1)}, bf16[1,1,8,8192]{3,2,1,0:T(8,128)(2,1)S(1)}, u32[]{:S(2)}, u32[]{:S(2)}) collective-permute-start(bf16[1,1,8,8192]{3,2,1,0:T(8,128)(2,1)} %get-tuple-element.21), channel_id=1, source_target_pairs={{0,3},{1,4},{2,5},{3,6},{4,7},{5,0},{6,1},{7,2},{8,11},{9,12},{10,... | collective-permute-start | bytes 393224 | tf_op jit(solution)/shard_map/ppermute | solution.py:25
  16.2 14.3 %collective-permute-start.10 = (bf16[1,1,8,8192]{3,2,1,0:T(8,128)(2,1)}, bf16[1,1,8,8192]{3,2,1,0:T(8,128)(2,1)S(1)}, u32[]{:S(2)}, u32[]{:S(2)}) collective-permute-start(bf16[1,1,8,8192]{3,2,1,0:T(8,128)(2,1)} %get-tuple-element.20), channel_id=1, source_target_pairs={{0,4},{1,5},{2,6},{3,7},{4,0},{5,1},{6,2},{7,3},{8,12},{9,13},{10,... | collective-permute-start | bytes 393224 | tf_op jit(solution)/shard_map/ppermute | solution.py:25
  16.7 14.5 %collective-permute-start.11 = (bf16[1,1,8,8192]{3,2,1,0:T(8,128)(2,1)}, bf16[1,1,8,8192]{3,2,1,0:T(8,128)(2,1)S(1)}, u32[]{:S(2)}, u32[]{:S(2)}) collective-permute-start(bf16[1,1,8,8192]{3,2,1,0:T(8,128)(2,1)} %get-tuple-element.19), channel_id=1, source_target_pairs={{0,5},{1,6},{2,7},{3,0},{4,1},{5,2},{6,3},{7,4},{8,13},{9,14},{10,... | collective-permute-start | bytes 393224 | tf_op jit(solution)/shard_map/ppermute | solution.py:25
  22.2 1.2 copy-start
  24.7 7.9 %collective-permute-start.12 = (bf16[1,1,8,8192]{3,2,1,0:T(8,128)(2,1)S(1)}, bf16[1,1,8,8192]{3,2,1,0:T(8,128)(2,1)S(1)}, u32[]{:S(2)}, u32[]{:S(2)}) collective-permute-start(bf16[1,1,8,8192]{3,2,1,0:T(8,128)(2,1)S(1)} %get-tuple-element.18), channel_id=1, source_target_pairs={{0,6},{1,7},{2,0},{3,1},{4,2},{5,3},{6,4},{7,5},{8,14},{9,15},{10,... | collective-permute-start | bytes 393224 | tf_op jit(solution)/shard_map/ppermute | solution.py:25
  27.1 7.2 %collective-permute-start.13 = (bf16[1,1,8,8192]{3,2,1,0:T(8,128)(2,1)S(1)}, bf16[1,1,8,8192]{3,2,1,0:T(8,128)(2,1)S(1)}, u32[]{:S(2)}, u32[]{:S(2)}) collective-permute-start(bf16[1,1,8,8192]{3,2,1,0:T(8,128)(2,1)S(1)} %get-tuple-element.17), channel_id=1, source_target_pairs={{0,7},{1,0},{2,1},{3,2},{4,3},{5,4},{6,5},{7,6},{8,15},{9,8},{10,9... | collective-permute-start | bytes 393224 | tf_op jit(solution)/shard_map/ppermute | solution.py:25
  30.5 6.2 %collective-permute-start = (bf16[1,1,8,8192]{3,2,1,0:T(8,128)(2,1)S(1)}, bf16[1,1,8,8192]{3,2,1,0:T(8,128)(2,1)S(1)}, u32[]{:S(2)}, u32[]{:S(2)}) collective-permute-start(bf16[1,1,8,8192]{3,2,1,0:T(8,128)(2,1)S(1)} %get-tuple-element.15), channel_id=1, source_target_pairs={{0,1},{1,2},{2,3},{3,4},{4,5},{5,6},{6,7},{7,0},{8,9},{9,10},{10,1... | collective-permute-start | bytes 393224 | tf_op jit(solution)/shard_map/ppermute | solution.py:25
  30.6 7.4 %collective-permute-start.1 = (bf16[1,1,8,8192]{3,2,1,0:T(8,128)(2,1)S(1)}, bf16[1,1,8,8192]{3,2,1,0:T(8,128)(2,1)S(1)}, u32[]{:S(2)}, u32[]{:S(2)}) collective-permute-start(bf16[1,1,8,8192]{3,2,1,0:T(8,128)(2,1)S(1)} %get-tuple-element.14), channel_id=1, source_target_pairs={{0,2},{1,3},{2,4},{3,5},{4,6},{5,7},{6,0},{7,1},{8,10},{9,11},{10,... | collective-permute-start | bytes 393224 | tf_op jit(solution)/shard_map/ppermute | solution.py:25
  31.2 11.5 %collective-permute-start.2 = (bf16[1,1,8,8192]{3,2,1,0:T(8,128)(2,1)S(1)}, bf16[1,1,8,8192]{3,2,1,0:T(8,128)(2,1)S(1)}, u32[]{:S(2)}, u32[]{:S(2)}) collective-permute-start(bf16[1,1,8,8192]{3,2,1,0:T(8,128)(2,1)S(1)} %get-tuple-element.13), channel_id=1, source_target_pairs={{0,3},{1,4},{2,5},{3,6},{4,7},{5,0},{6,1},{7,2},{8,11},{9,12},{10,... | collective-permute-start | bytes 393224 | tf_op jit(solution)/shard_map/ppermute | solution.py:25
  32.7 10.3 %collective-permute-start.3 = (bf16[1,1,8,8192]{3,2,1,0:T(8,128)(2,1)S(1)}, bf16[1,1,8,8192]{3,2,1,0:T(8,128)(2,1)S(1)}, u32[]{:S(2)}, u32[]{:S(2)}) collective-permute-start(bf16[1,1,8,8192]{3,2,1,0:T(8,128)(2,1)S(1)} %get-tuple-element.12), channel_id=1, source_target_pairs={{0,4},{1,5},{2,6},{3,7},{4,0},{5,1},{6,2},{7,3},{8,12},{9,13},{10,... | collective-permute-start | bytes 393224 | tf_op jit(solution)/shard_map/ppermute | solution.py:25
  34.3 9.2 %collective-permute-start.4 = (bf16[1,1,8,8192]{3,2,1,0:T(8,128)(2,1)S(1)}, bf16[1,1,8,8192]{3,2,1,0:T(8,128)(2,1)S(1)}, u32[]{:S(2)}, u32[]{:S(2)}) collective-permute-start(bf16[1,1,8,8192]{3,2,1,0:T(8,128)(2,1)S(1)} %get-tuple-element.11), channel_id=1, source_target_pairs={{0,5},{1,6},{2,7},{3,0},{4,1},{5,2},{6,3},{7,4},{8,13},{9,14},{10,... | collective-permute-start | bytes 393224 | tf_op jit(solution)/shard_map/ppermute | solution.py:25
  36.7 7.4 %collective-permute-start.5 = (bf16[1,1,8,8192]{3,2,1,0:T(8,128)(2,1)}, bf16[1,1,8,8192]{3,2,1,0:T(8,128)(2,1)S(1)}, u32[]{:S(2)}, u32[]{:S(2)}) collective-permute-start(bf16[1,1,8,8192]{3,2,1,0:T(8,128)(2,1)} %get-tuple-element.10), channel_id=1, source_target_pairs={{0,6},{1,7},{2,0},{3,1},{4,2},{5,3},{6,4},{7,5},{8,14},{9,15},{10,... | collective-permute-start | bytes 393224 | tf_op jit(solution)/shard_map/ppermute | solution.py:25
  38.0 149.4 %collective-permute-start.6 = (bf16[1,1,8,8192]{3,2,1,0:T(8,128)(2,1)S(1)}, bf16[1,1,8,8192]{3,2,1,0:T(8,128)(2,1)S(1)}, u32[]{:S(2)}, u32[]{:S(2)}) collective-permute-start(bf16[1,1,8,8192]{3,2,1,0:T(8,128)(2,1)S(1)} %get-tuple-element.9), channel_id=1, source_target_pairs={{0,7},{1,0},{2,1},{3,2},{4,3},{5,4},{6,5},{7,6},{8,15},{9,8},{10,9... | collective-permute-start | bytes 393224 | tf_op jit(solution)/shard_map/ppermute | solution.py:25
  183.6 19.1 %all-to-all-start.1 = ((bf16[1,8,8,8192]{3,2,0,1:T(8,128)(2,1)}), bf16[1,8,8,8192]{3,2,0,1:T(8,128)(2,1)S(1)}, u32[]{:S(2)}, u32[]{:S(2)}) async-start(bf16[1,8,8,8192]{3,2,0,1:T(8,128)(2,1)} %fusion.3), calls=%async_computation.1 | async-start | bytes 2097152 | tf_op jit(solution)/shard_map/all_to_all | solution.py:55
  202.7 18.9 %all-to-all-start = ((bf16[1,8,8,8192]{3,2,0,1:T(8,128)(2,1)}), bf16[1,8,8,8192]{3,2,0,1:T(8,128)(2,1)S(1)}, u32[]{:S(2)}, u32[]{:S(2)}) async-start(bf16[1,8,8,8192]{3,2,0,1:T(8,128)(2,1)} %fusion.1), calls=%async_computation | async-start | bytes 2097152 | tf_op jit(solution)/shard_map/all_to_all | solution.py:55
Sparse Core Ops, SparseCore 0:
  22.3 157.4 all-reduce.2
